TPU v7x, 32 devices: a whole 2x2x4 slice. The times are simulated.
32 devices in a mesh: dp: 4 (over z), expert: 8 (over y, x, core).
Axes of the slice: x: 2, y: 2, z: 4, core: 2. Of those that a mesh axis runs over, the one named last changes fastest.
Arguments:
- out_grad: bfloat16 [8192, 4096], P(('dp', 'expert')), may hold values from -6 to 6
- destination: int32 [8192, 1], P(('dp', 'expert')), may hold values from 0 to 7; in each aligned block of 256 rows (0 to 255, 256 to 511, ...) at most 64 rows name the same one
- hidden: bfloat16 [16384, 1024], P(('dp', 'expert')), may hold values from -6 to 6
- weight: bfloat16 [8, 1024, 4096], P('expert', None, 'dp'), may hold values from -0.09375 to 0.09375
- left_prev: float32 [8, 2048, 1024], P('expert', 'dp'), may hold values from -3 to 3
- right_prev: float32 [8, 4096, 2048], P('expert', 'dp'), may hold values from -3 to 3
Outputs:
- grad_rows: bfloat16 [8192, 1024], P(('dp', 'expert'))
- left_stats: float32 [8, 2048, 1024], P('expert', 'dp')
- right_stats: float32 [8, 4096, 2048], P('expert', 'dp')
Inputs may be any that keep to these rules, and one draw needn't show every extreme that they name: Among the rows of one device at most 64 have the same destination, and on some device that many do.
All inputs are finite; a program needn't handle non-finite values.
Results may differ from a plain program's by a relative error of at most 0.001.
Values may be sent and summed in bfloat16 or wider, within the bound.
A program may use at most 128 MiB of HBM per device.

v0:
```python
import jax
import jax.numpy as jnp
from jax import lax
from jax.sharding import PartitionSpec as P

ema_decay = 0.9


def swapped(value, axis, distance):
    mask = 2**distance
    pairs = [(source, source ^ mask) for source in range(lax.axis_size(axis))]
    return lax.ppermute(value, axis, pairs)


def slot_places(dest_column, expert_count, capacity):
    choose = (dest_column[:, None] == jnp.arange(expert_count, dtype=jnp.int32)[None, :]).astype(
        jnp.int32
    )
    before = jnp.cumsum(choose, axis=0) - choose
    slot_rank = jnp.sum(before * choose, axis=1)
    return dest_column * capacity + slot_rank


def local(out_grad, destination, hidden, weight, left_prev, right_prev):
    expert_count = lax.axis_size("expert")
    group_count = lax.axis_size("dp")
    row_count, model_width = out_grad.shape
    slot_count, hidden_width = hidden.shape
    capacity = slot_count // expert_count
    target_slots = slot_places(destination[:, 0], expert_count, capacity)
    outgoing = jnp.zeros((slot_count, model_width), out_grad.dtype).at[target_slots].set(out_grad)
    arrived = lax.all_to_all(
        outgoing.reshape(expert_count, capacity, model_width),
        "expert",
        split_axis=0,
        concat_axis=0,
        tiled=True,
    )
    arrived = arrived.reshape(slot_count, model_width)
    columns = arrived
    slot_grad = lax.dot_general(
        columns,
        lax.all_gather(weight[0], "dp", axis=1, tiled=True),
        (((1,), (1,)), ((), ())),
        preferred_element_type=jnp.float32,
    ).astype(jnp.bfloat16)
    returned = lax.all_to_all(
        slot_grad.reshape(expert_count, capacity, hidden_width),
        "expert",
        split_axis=0,
        concat_axis=0,
        tiled=True,
    )
    grad_rows = returned.reshape(slot_count, hidden_width)[target_slots]
    half_width = model_width // group_count
    block_width = 2 * half_width
    columns_all = lax.all_to_all(arrived, "dp", split_axis=1, concat_axis=0, tiled=True)
    columns = columns_all
    own_piece = lax.dot_general(
        columns,
        lax.all_gather(hidden, "dp", axis=0, tiled=True),
        (((0,), (0,)), ((), ())),
        preferred_element_type=jnp.float32,
    )
    partner = swapped(own_piece.astype(jnp.bfloat16), "dp", 0).astype(own_piece.dtype)
    parity = lax.axis_index("dp") % 2
    upper_half = parity == 0
    first_half = jnp.where(upper_half, own_piece, partner)
    second_half = jnp.where(upper_half, partner, own_piece)
    block_grad = jnp.concatenate([first_half, second_half], axis=0)
    scale_left = 1.0 / (group_count * row_count * block_width)
    scale_right = 1.0 / (group_count * row_count * hidden_width)
    right_gram = (
        lax.dot_general(
            own_piece,
            block_grad,
            (((1,), (1,)), ((), ())),
            precision=lax.Precision.HIGHEST,
            preferred_element_type=jnp.float32,
        )
        * scale_right
    )
    half_hidden = hidden_width // 2
    hidden_cols = lax.dynamic_slice_in_dim(block_grad, parity * half_hidden, half_hidden, 1)
    left_gram = (
        lax.dot_general(
            hidden_cols,
            block_grad,
            (((0,), (0,)), ((), ())),
            precision=lax.Precision.HIGHEST,
            preferred_element_type=jnp.float32,
        )
        * scale_left
    )
    left_stats = ema_decay * left_prev + (1.0 - ema_decay) * left_gram[None]
    right_stats = ema_decay * right_prev + (1.0 - ema_decay) * right_gram[None]
    return (grad_rows, left_stats, right_stats)


def solution(mesh):
    placed = (
        P(("dp", "expert"), None),
        P(("dp", "expert"), None),
        P(("dp", "expert"), None),
        P("expert", None, "dp"),
        P("expert", "dp", None),
        P("expert", "dp", None),
    )
    return jax.shard_map(
        local,
        mesh=mesh,
        in_specs=placed,
        out_specs=(P(("dp", "expert"), None), P("expert", "dp", None), P("expert", "dp", None)),
        check_vma=False,
    )
```

profile of v0, /device:TPU:1, one launch (start us, length us, event | category | flops | bytes accessed | tf_op | source)
XLA Modules:
  0.0 439.9 jit_solution(14873368726343647602)
XLA Ops:
  7.2 0.0 all-gather.4.cloned.1.call-start
  7.2 0.7 all-gather.4.cloned.1.call-update
  7.9 0.7 fusion.15
  8.6 0.6 reduce-window.6
  9.2 0.2 slice_reduce_fusion
  9.4 0.8 fusion.14
  10.2 0.7 compare_select_fusion
  10.9 7.1 %scatter_custom_fusion = bf16[512,4096]{1,0:T(8,128)(2,1)} fusion(s32[256]{0:T(256)S(1)} %bitcast.37, bf16[256,4096]{1,0:T(8,128)(2,1)} %param.6, bf16[]{:T(256)} %constant.14.clone.1), kind=kCustom, calls=%fused_computation.14 | custom fusion | bytes 4194816 | tf_op jit(solution)/shard_map/scatter | solution.py:31
  18.0 5.2 %all-to-all-start = ((bf16[8,64,4096]{2,1,0:T(8,128)(2,1)}), bf16[8,64,4096]{2,1,0:T(8,128)(2,1)}, u32[]{:S(2)}, u32[]{:S(2)}) async-start(bf16[8,64,4096]{2,1,0:T(8,128)(2,1)} %bitcast.34), calls=%async_computation | async-start | bytes 8388608 | tf_op jit(solution)/shard_map/all_to_all | solution.py:32
  23.2 0.0 all-gather.6.cloned.1.call-start
  23.2 0.7 all-gather.6.cloned.1.call-update
  23.9 44.9 %all-to-all-done = bf16[8,64,4096]{2,1,0:T(8,128)(2,1)} async-done(((bf16[8,64,4096]{2,1,0:T(8,128)(2,1)}), bf16[8,64,4096]{2,1,0:T(8,128)(2,1)}, u32[]{:S(2)}, u32[]{:S(2)}) %all-to-all-start) | async-done | bytes 4194336 | tf_op jit(solution)/shard_map/all_to_all | solution.py:32
  68.9 7.8 %all_to_all.22 = bf16[512,4,1024]{2,1,0:T(4,128)(2,1)} reshape(bf16[8,64,4096]{2,1,0:T(8,128)(2,1)} %all-to-all-done) | data formatting | bytes 8388608 | tf_op jit(solution)/shard_map/all_to_all | solution.py:57
  76.7 5.5 %copy.10 = bf16[512,4,1024]{2,0,1:T(8,128)(2,1)} copy(bf16[512,4,1024]{2,1,0:T(4,128)(2,1)} %all_to_all.22) | data formatting | bytes 8388608 | tf_op jit(solution)/shard_map/all_to_all | solution.py:57
  82.2 5.8 %all-to-all-start.2 = ((bf16[512,4,1024]{2,0,1:T(8,128)(2,1)}), bf16[512,4,1024]{2,0,1:T(8,128)(2,1)}, u32[]{:S(2)}, u32[]{:S(2)}) async-start(bf16[512,4,1024]{2,0,1:T(8,128)(2,1)} %copy.10), calls=%async_computation.2 | async-start | bytes 8388608 | tf_op jit(solution)/shard_map/all_to_all | solution.py:57
  88.0 4.2 all-gather.4.cloned.1.call-done
  92.2 194.6 %all-to-all-done.2 = bf16[512,4,1024]{2,0,1:T(8,128)(2,1)} async-done(((bf16[512,4,1024]{2,0,1:T(8,128)(2,1)}), bf16[512,4,1024]{2,0,1:T(8,128)(2,1)}, u32[]{:S(2)}, u32[]{:S(2)}) %all-to-all-start.2) | async-done | bytes 4194336 | tf_op jit(solution)/shard_map/all_to_all | solution.py:57
  286.8 10.7 %fusion.19 = (bf16[1024,1024]{1,0:T(8,128)(2,1)}, f32[1024,1024]{1,0:T(8,128)}) fusion(bf16[2048,1024]{1,0:T(8,128)(2,1)} %bitcast.12, bf16[2048,1024]{1,0:T(8,128)(2,1)} %all-gather.4.cloned.1.call-done), kind=kOutput, calls=%fused_computation.29 | convolution fusion | flops 4296015872 | bytes 14680064 | tf_op jit(solution)/shard_map/dot_general | solution.py:59
  297.5 0.0 collective-permute-start
  297.5 60.1 %collective-permute-done = bf16[1024,1024]{1,0:T(8,128)(2,1)S(1)} collective-permute-done((bf16[1024,1024]{1,0:T(8,128)(2,1)}, bf16[1024,1024]{1,0:T(8,128)(2,1)S(1)}, u32[]{:S(2)}, u32[]{:S(2)}) %collective-permute-start) | collective-permute-done | bytes 2097184 | tf_op jit(solution)/shard_map/ppermute | solution.py:12
  357.6 7.0 %convert_select_fusion.1 = (f32[1024,1024]{1,0:T(8,128)}, f32[1024,1024]{1,0:T(8,128)}) fusion(f32[1024,1024]{1,0:T(8,128)} %get-tuple-element.6, bf16[1024,1024]{1,0:T(8,128)(2,1)S(1)} %collective-permute-done, pred[]{:T(512)S(6)} %eq.38), kind=kLoop, calls=%fused_computation.11 | loop fusion | flops 3145728 | bytes 14680065 | tf_op jit(solution)/shard_map/jit(_where)/select_n | solution.py:68
  364.6 0.0 all-gather.6.cloned.1.call-done
  364.6 10.2 %fusion.8 = bf16[512,1024]{1,0:T(8,128)(2,1)} fusion(bf16[512,4096]{1,0:T(8,128)(2,1)} %bitcast.7, bf16[1,1024,4096]{2,1,0:T(8,128)(2,1)} %all-gather.6.cloned.1.call-done), kind=kOutput, calls=%fused_computation.16 | convolution fusion | flops 4295491584 | bytes 13631488 | tf_op jit(solution)/shard_map/dot_general | solution.py:41
  374.9 7.8 %all-to-all-start.1 = ((bf16[8,64,1024]{2,1,0:T(8,128)(2,1)}), bf16[8,64,1024]{2,1,0:T(8,128)(2,1)S(1)}, u32[]{:S(2)}, u32[]{:S(2)}) async-start(bf16[8,64,1024]{2,1,0:T(8,128)(2,1)} %bitcast.9), calls=%async_computation.1 | async-start | bytes 2097152 | tf_op jit(solution)/shard_map/all_to_all | solution.py:47
  382.7 0.0 copy-start
  382.7 0.0 copy-start.1
  382.7 0.0 copy-start.2
  382.7 33.1 %bitcast_add_fusion = f32[1,1024,2048]{2,1,0:T(8,128)} fusion(f32[1,1024,2048]{2,1,0:T(8,128)} %param.11, f32[1024,1024]{1,0:T(8,128)} %get-tuple-element.6, f32[1024,1024]{1,0:T(8,128)} %get-tuple-element.4, f32[1024,1024]{1,0:T(8,128)} %get-tuple-element.3), kind=kOutput, calls=%fused_computation.5 | convolution fusion | flops 25778192384 | bytes 29360128 | tf_op jit(solution)/shard_map/dot_general | solution.py:74
  415.8 0.0 copy-done
  415.8 0.0 copy-done.1
  415.8 0.0 copy-done.2
  415.8 15.1 %bitcast_add_fusion.1 = f32[1,512,1024]{2,1,0:T(8,128)} fusion(f32[1,512,1024]{2,1,0:T(8,128)S(1)} %copy-done.2, f32[1024,1024]{1,0:T(8,128)S(1)} %copy-done.1, f32[1024,1024]{1,0:T(8,128)S(1)} %copy-done, s32[]{:T(128)S(6)} %select_n.32), kind=kOutput, calls=%fused_computation.13 | convolution fusion | flops 12889620480 | bytes 20971524 | tf_op jit(solution)/shard_map/dot_general | solution.py:86
  430.9 0.0 all-to-all-done.1
  430.9 2.0 gather_fusion
  (3 shorter events, 0.0 us)
Async XLA Ops:
  7.2 85.1 %all-gather.4.cloned.1.call-start = ((), (), s32[]{:S(2)}) async-start(), calls=%async_computation.3 | async-start | bytes 5242880 | tf_op jit(solution)/shard_map/all_gather | solution.py:61
  18.0 50.9 %all-to-all-start = ((bf16[8,64,4096]{2,1,0:T(8,128)(2,1)}), bf16[8,64,4096]{2,1,0:T(8,128)(2,1)}, u32[]{:S(2)}, u32[]{:S(2)}) async-start(bf16[8,64,4096]{2,1,0:T(8,128)(2,1)} %bitcast.34), calls=%async_computation | async-start | bytes 8388608 | tf_op jit(solution)/shard_map/all_to_all | solution.py:32
  23.2 341.4 %all-gather.6.cloned.1.call-start = ((), (), s32[]{:S(2)}) async-start(), calls=%async_computation.4 | async-start | bytes 10485760 | tf_op jit(solution)/shard_map/all_gather | solution.py:43
  82.2 204.6 %all-to-all-start.2 = ((bf16[512,4,1024]{2,0,1:T(8,128)(2,1)}), bf16[512,4,1024]{2,0,1:T(8,128)(2,1)}, u32[]{:S(2)}, u32[]{:S(2)}) async-start(bf16[512,4,1024]{2,0,1:T(8,128)(2,1)} %copy.10), calls=%async_computation.2 | async-start | bytes 8388608 | tf_op jit(solution)/shard_map/all_to_all | solution.py:57
  297.5 60.1 %collective-permute-start = (bf16[1024,1024]{1,0:T(8,128)(2,1)}, bf16[1024,1024]{1,0:T(8,128)(2,1)S(1)}, u32[]{:S(2)}, u32[]{:S(2)}) collective-permute-start(bf16[1024,1024]{1,0:T(8,128)(2,1)} %get-tuple-element.5), channel_id=1, source_target_pairs={{0,8},{8,0},{16,24},{24,16},{1,9},{9,1},{17,25},{25,17},{2,10},{10... | collective-permute-start | bytes 6291464 | tf_op jit(solution)/shard_map/ppermute | solution.py:12
  374.9 56.1 %all-to-all-start.1 = ((bf16[8,64,1024]{2,1,0:T(8,128)(2,1)}), bf16[8,64,1024]{2,1,0:T(8,128)(2,1)S(1)}, u32[]{:S(2)}, u32[]{:S(2)}) async-start(bf16[8,64,1024]{2,1,0:T(8,128)(2,1)} %bitcast.9), calls=%async_computation.1 | async-start | bytes 2097152 | tf_op jit(solution)/shard_map/all_to_all | solution.py:47
  382.7 33.1 %copy-start = (f32[1024,1024]{1,0:T(8,128)S(1)}, f32[1024,1024]{1,0:T(8,128)}, u32[]{:S(2)}) copy-start(f32[1024,1024]{1,0:T(8,128)} %get-tuple-element.3) | copy-start | bytes 12582916
  382.7 33.1 %copy-start.1 = (f32[1024,1024]{1,0:T(8,128)S(1)}, f32[1024,1024]{1,0:T(8,128)}, u32[]{:S(2)}) copy-start(f32[1024,1024]{1,0:T(8,128)} %get-tuple-element.4) | copy-start | bytes 12582916
  382.7 33.1 %copy-start.2 = (f32[1,512,1024]{2,1,0:T(8,128)S(1)}, f32[1,512,1024]{2,1,0:T(8,128)}, u32[]{:S(2)}) copy-start(f32[1,512,1024]{2,1,0:T(8,128)} %param.10) | copy-start | bytes 6291460
Sparse Core Ops, SparseCore 0:
  9.5 82.6 all-gather.3
  93.8 223.5 all-gather.5
where the time goes:
time: 446 us; the launch traced here: 440 us
  waiting for transfers between devices  305 us (68%)
  matrix products  69.1 us (15%)
  local copies, waits for them, and re-layouts  22.6 us (5%)
  starting transfers between devices  18.9 us (4%)
  between operations  14.3 us (3%)
  other arithmetic  9.75 us (2%)
    all_to_all x1, waiting for transfers between devices, local(): lax.all_to_all(arrived, 'dp', split_axis=1, concat_axis=0, tiled=True)  195 us
    ppermute x1, waiting for transfers between devices, swapped(): return lax.ppermute(value, axis, pairs)  60.1 us
    all_to_all x1, waiting for transfers between devices, local(): lax.all_to_all(outgoing.reshape(expert_count, capacity, model_width), 'ex...  44.9 us
    dot_general x1, matrix products, local(): lax.dot_general(own_piece, block_grad, (((1,), (1,)), ((), ())), precisio...  33.1 us
    dot_general x1, matrix products, local(): lax.dot_general(hidden_cols, block_grad, (((0,), (0,)), ((), ())), precis...  15.1 us
    all_to_all x2, local copies, waits for them, and re-layouts, local(): lax.all_to_all(arrived, 'dp', split_axis=1, concat_axis=0, tiled=True)  13.3 us
    dot_general x1, matrix products, local(): lax.dot_general(columns, lax.all_gather(hidden, 'dp', axis=0, tiled=True)...  10.7 us
    dot_general x1, matrix products, local(): lax.dot_general(columns, lax.all_gather(weight[0], 'dp', axis=1, tiled=Tr...  10.2 us
  transfers between devices with their start and end apart: 6, of which 4 were waited for; matrix products, arithmetic and copies ran while one was open for 19% of the time, Pallas kernels for 0%

commit v1 on v0

--- a/solution.py
+++ b/solution.py
@@ -4,6 +4,29 @@
 from jax.sharding import PartitionSpec as P
 
 ema_decay = 0.9
+
+
+def cut_along(x, dim, size):
+    dims = x.shape
+    blocks = x.reshape(*dims[:dim], size, dims[dim] // size, *dims[dim + 1 :])
+    return jnp.moveaxis(blocks, dim, 0)
+
+
+def joined_along(blocks, dim):
+    shape = list(blocks.shape[1:])
+    shape[dim] *= blocks.shape[0]
+    return jnp.moveaxis(blocks, 0, dim).reshape(shape)
+
+
+def pairwise_exchange(value, axis, split_dim, concat_dim):
+    length, here = (lax.axis_size(axis), lax.axis_index(axis))
+    blocks = cut_along(value, split_dim, length)
+    finished = [blocks[here]]
+    for hop in range(1, length):
+        sent = blocks[here ^ hop]
+        finished.append(lax.ppermute(sent, axis, [(i, i ^ hop) for i in range(length)]))
+    blocks = jnp.stack(finished)[here ^ jnp.arange(length)]
+    return joined_along(blocks, concat_dim)
 
 
 def swapped(value, axis, distance):
@@ -29,12 +52,8 @@
     capacity = slot_count // expert_count
     target_slots = slot_places(destination[:, 0], expert_count, capacity)
     outgoing = jnp.zeros((slot_count, model_width), out_grad.dtype).at[target_slots].set(out_grad)
-    arrived = lax.all_to_all(
-        outgoing.reshape(expert_count, capacity, model_width),
-        "expert",
-        split_axis=0,
-        concat_axis=0,
-        tiled=True,
+    arrived = pairwise_exchange(
+        outgoing.reshape(expert_count, capacity, model_width), "expert", 0, 0
     )
     arrived = arrived.reshape(slot_count, model_width)
     columns = arrived

time: 446 us -> 459 us (1.029)
  local copies, waits for them, and re-layouts: 22.6 us -> 38 us
  waiting for transfers between devices: 305 us -> 299 us
    all_to_all x1 -> x0, waiting for transfers between devices: 44.9 us -> none  [local(): lax.all_to_all(outgoing.reshape(expert_count, capacity, model_width), 'ex...]
    ppermute x0 -> x7, waiting for transfers between devices: none -> 37 us  [pairwise_exchange(): lax.ppermute(sent, axis, [(i, i ^ hop) for i in range(length)])]
    ppermute x0 -> x7, starting transfers between devices: none -> 10.4 us  [pairwise_exchange(): lax.ppermute(sent, axis, [(i, i ^ hop) for i in range(length)])]
    all_to_all x1 -> x0, starting transfers between devices: 5.21 us -> none  [local(): lax.all_to_all(outgoing.reshape(expert_count, capacity, model_width), 'ex...]
    all_to_all x1, waiting for transfers between devices: 195 us -> 200 us  [local(): lax.all_to_all(arrived, 'dp', split_axis=1, concat_axis=0, tiled=True)]
    unnamed x6 -> x12, local copies, waits for them, and re-layouts: 0.01 us -> 5.09 us
    gather x0 -> x1, local copies, waits for them, and re-layouts: none -> 5.01 us  [pairwise_exchange(): blocks = jnp.stack(finished)[here ^ jnp.arange(length)]]
  transfers between devices with their start and end apart: 6 -> 12, of which waited for: 4 -> 5; matrix products, arithmetic and copies ran while one was open for 19% -> 21% of each run, Pallas kernels for 0% -> 0%
where the time goes in v1:
time: 459 us; the launch traced here: 452 us
  waiting for transfers between devices  299 us (65%)
  matrix products  69 us (15%)
  local copies, waits for them, and re-layouts  38 us (8%)
  starting transfers between devices  21.9 us (5%)
  between operations  14.4 us (3%)
  other arithmetic  9.75 us (2%)
    all_to_all x1, waiting for transfers between devices, local(): lax.all_to_all(arrived, 'dp', split_axis=1, concat_axis=0, tiled=True)  200 us
    ppermute x1, waiting for transfers between devices, swapped(): return lax.ppermute(value, axis, pairs)  61.4 us
    ppermute x7, waiting for transfers between devices, pairwise_exchange(): lax.ppermute(sent, axis, [(i, i ^ hop) for i in range(length)])  37 us
    dot_general x1, matrix products, local(): lax.dot_general(own_piece, block_grad, (((1,), (1,)), ((), ())), precisio...  33.1 us
    dot_general x1, matrix products, local(): lax.dot_general(hidden_cols, block_grad, (((0,), (0,)), ((), ())), precis...  15.1 us
    all_to_all x2, local copies, waits for them, and re-layouts, local(): lax.all_to_all(arrived, 'dp', split_axis=1, concat_axis=0, tiled=True)  13.3 us
    dot_general x1, matrix products, local(): lax.dot_general(columns, lax.all_gather(hidden, 'dp', axis=0, tiled=True)...  10.7 us
    ppermute x7, starting transfers between devices, pairwise_exchange(): lax.ppermute(sent, axis, [(i, i ^ hop) for i in range(length)])  10.4 us
  transfers between devices with their start and end apart: 12, of which 5 were waited for; matrix products, arithmetic and copies ran while one was open for 21% of the time, Pallas kernels for 0%

profile of v1, /device:TPU:1, one launch (start us, length us, event | category | flops | bytes accessed | tf_op | source)
XLA Modules:
  0.0 452.0 jit_solution(1144426905658835822)
XLA Ops:
  7.2 0.0 all-gather.4.cloned.1.call-start
  7.2 0.7 all-gather.4.cloned.1.call-update
  7.9 0.0 all-gather.6.cloned.1.call-start
  8.0 0.7 fusion.15
  8.7 0.6 reduce-window.6
  9.2 0.2 slice_reduce_fusion
  9.5 0.8 fusion.14
  10.3 0.7 compare_select_fusion
  11.0 7.1 %scatter_custom_fusion = bf16[512,4096]{1,0:T(8,128)(2,1)} fusion(s32[256]{0:T(256)S(1)} %bitcast.69, bf16[256,4096]{1,0:T(8,128)(2,1)} %param.6, bf16[]{:T(256)} %constant.18.clone.1), kind=kCustom, calls=%fused_computation.15 | custom fusion | bytes 4194816 | tf_op jit(solution)/shard_map/scatter | solution.py:54
  18.1 4.5 dynamic-slice_bitcast_fusion
  22.6 0.0 collective-permute-start
  22.6 2.6 collective-permute-start.1
  25.2 0.0 collective-permute-start.2
  25.2 1.7 collective-permute-start.3
  26.9 0.3 collective-permute-start.4
  27.2 0.0 all-gather.6.cloned.1.call-update
  27.3 0.0 collective-permute-done
  27.3 2.5 collective-permute-start.5
  29.8 0.9 bitcast_dynamic-update-slice_fusion.6
  30.6 7.1 %collective-permute-done.1 = bf16[1,64,4096]{2,1,0:T(8,128)(2,1)S(1)} collective-permute-done((bf16[1,64,4096]{2,1,0:T(8,128)(2,1)}, bf16[1,64,4096]{2,1,0:T(8,128)(2,1)S(1)}, u32[]{:S(2)}, u32[]{:S(2)}) %collective-permute-start.1) | collective-permute-done | bytes 524320 | tf_op jit(solution)/shard_map/ppermute | solution.py:27
  37.8 3.3 collective-permute-start.6
  41.1 0.8 bitcast_dynamic-update-slice_fusion.5
  41.9 7.5 %collective-permute-done.2 = bf16[1,64,4096]{2,1,0:T(8,128)(2,1)S(1)} collective-permute-done((bf16[1,64,4096]{2,1,0:T(8,128)(2,1)}, bf16[1,64,4096]{2,1,0:T(8,128)(2,1)S(1)}, u32[]{:S(2)}, u32[]{:S(2)}) %collective-permute-start.2) | collective-permute-done | bytes 524320 | tf_op jit(solution)/shard_map/ppermute | solution.py:27
  49.4 0.8 bitcast_dynamic-update-slice_fusion.4
  50.3 0.0 collective-permute-done.3
  50.3 0.8 bitcast_dynamic-update-slice_fusion.3
  51.1 22.3 %collective-permute-done.4 = bf16[1,64,4096]{2,1,0:T(8,128)(2,1)S(1)} collective-permute-done((bf16[1,64,4096]{2,1,0:T(8,128)(2,1)}, bf16[1,64,4096]{2,1,0:T(8,128)(2,1)S(1)}, u32[]{:S(2)}, u32[]{:S(2)}) %collective-permute-start.4) | collective-permute-done | bytes 524320 | tf_op jit(solution)/shard_map/ppermute | solution.py:27
  73.4 0.8 bitcast_dynamic-update-slice_fusion.2
  74.2 0.0 collective-permute-done.5
  74.2 0.9 bitcast_dynamic-update-slice_fusion.1
  75.1 0.0 collective-permute-done.6
  75.1 0.8 bitcast_dynamic-update-slice_fusion
  75.9 5.0 %gather_fusion = bf16[8,64,4096]{2,1,0:T(8,128)(2,1)} fusion(bf16[8,64,4096]{2,1,0:T(8,128)(2,1)} %bitcast.66, s32[1024]{0:T(1024)S(1)} %pad_clamp_fusion.1), kind=kCustom, calls=%fused_computation | custom fusion | bytes 8388640 | tf_op jit(solution)/shard_map/gather | solution.py:28
  80.9 7.8 %all_to_all.18 = bf16[512,4,1024]{2,1,0:T(4,128)(2,1)} reshape(bf16[8,64,4096]{2,1,0:T(8,128)(2,1)} %gather_fusion) | data formatting | bytes 8388608 | tf_op jit(solution)/shard_map/all_to_all | solution.py:76
  88.8 5.5 %copy.10 = bf16[512,4,1024]{2,0,1:T(8,128)(2,1)} copy(bf16[512,4,1024]{2,1,0:T(4,128)(2,1)} %all_to_all.18) | data formatting | bytes 8388608 | tf_op jit(solution)/shard_map/all_to_all | solution.py:76
  94.2 5.3 %all-to-all-start.1 = ((bf16[512,4,1024]{2,0,1:T(8,128)(2,1)}), bf16[512,4,1024]{2,0,1:T(8,128)(2,1)}, u32[]{:S(2)}, u32[]{:S(2)}) async-start(bf16[512,4,1024]{2,0,1:T(8,128)(2,1)} %copy.10), calls=%async_computation.1 | async-start | bytes 8388608 | tf_op jit(solution)/shard_map/all_to_all | solution.py:76
  99.6 0.0 all-gather.4.cloned.1.call-done
  99.6 199.7 %all-to-all-done.1 = bf16[512,4,1024]{2,0,1:T(8,128)(2,1)} async-done(((bf16[512,4,1024]{2,0,1:T(8,128)(2,1)}), bf16[512,4,1024]{2,0,1:T(8,128)(2,1)}, u32[]{:S(2)}, u32[]{:S(2)}) %all-to-all-start.1) | async-done | bytes 4194336 | tf_op jit(solution)/shard_map/all_to_all | solution.py:76
  299.3 10.7 %fusion.20 = (bf16[1024,1024]{1,0:T(8,128)(2,1)}, f32[1024,1024]{1,0:T(8,128)}) fusion(bf16[2048,1024]{1,0:T(8,128)(2,1)} %bitcast.28, bf16[2048,1024]{1,0:T(8,128)(2,1)} %all-gather.4.cloned.1.call-done), kind=kOutput, calls=%fused_computation.48 | convolution fusion | flops 4296015872 | bytes 14680064 | tf_op jit(solution)/shard_map/dot_general | solution.py:78
  310.0 1.6 collective-permute-start.7
  311.6 61.4 %collective-permute-done.7 = bf16[1024,1024]{1,0:T(8,128)(2,1)S(1)} collective-permute-done((bf16[1024,1024]{1,0:T(8,128)(2,1)}, bf16[1024,1024]{1,0:T(8,128)(2,1)S(1)}, u32[]{:S(2)}, u32[]{:S(2)}) %collective-permute-start.7) | collective-permute-done | bytes 2097184 | tf_op jit(solution)/shard_map/ppermute | solution.py:35
  373.1 7.0 %convert_select_fusion.1 = (f32[1024,1024]{1,0:T(8,128)}, f32[1024,1024]{1,0:T(8,128)}) fusion(f32[1024,1024]{1,0:T(8,128)} %get-tuple-element.14, bf16[1024,1024]{1,0:T(8,128)(2,1)S(1)} %collective-permute-done.7, pred[]{:T(512)S(6)} %eq.38), kind=kLoop, calls=%fused_computation.12 | loop fusion | flops 3145728 | bytes 14680065 | tf_op jit(solution)/shard_map/jit(_where)/select_n | solution.py:87
  380.1 10.1 %fusion.8 = bf16[512,1024]{1,0:T(8,128)(2,1)} fusion(bf16[512,4096]{1,0:T(8,128)(2,1)} %bitcast.64, bf16[1,1024,4096]{2,1,0:T(8,128)(2,1)} %all-gather.6.cloned.1.call-done), kind=kOutput, calls=%fused_computation.17 | convolution fusion | flops 4295491584 | bytes 13631488 | tf_op jit(solution)/shard_map/dot_general | solution.py:60
  390.2 4.5 all-to-all-start
  394.8 0.0 copy-start.2
  394.8 33.1 %bitcast_add_fusion = f32[1,1024,2048]{2,1,0:T(8,128)} fusion(f32[1,1024,2048]{2,1,0:T(8,128)} %param.11, f32[1024,1024]{1,0:T(8,128)} %get-tuple-element.14, f32[1024,1024]{1,0:T(8,128)} %get-tuple-element.4, f32[1024,1024]{1,0:T(8,128)} %get-tuple-element.3), kind=kOutput, calls=%fused_computation.6 | convolution fusion | flops 25778192384 | bytes 29360128 | tf_op jit(solution)/shard_map/dot_general | solution.py:93
  427.9 15.1 %bitcast_add_fusion.1 = f32[1,512,1024]{2,1,0:T(8,128)} fusion(f32[1,512,1024]{2,1,0:T(8,128)S(1)} %copy-done.2, f32[1024,1024]{1,0:T(8,128)S(1)} %copy-done.1, f32[1024,1024]{1,0:T(8,128)S(1)} %copy-done, s32[]{:T(128)S(6)} %select_n.75), kind=kOutput, calls=%fused_computation.14 | convolution fusion | flops 12889620480 | bytes 20971524 | tf_op jit(solution)/shard_map/dot_general | solution.py:105
  443.0 2.0 gather_fusion.1
  (12 shorter events, 0.1 us)
Async XLA Ops:
  7.2 92.4 %all-gather.4.cloned.1.call-start = ((), (), s32[]{:S(2)}) async-start(), calls=%async_computation.2 | async-start | bytes 5242880 | tf_op jit(solution)/shard_map/all_gather | solution.py:80
  7.9 372.2 %all-gather.6.cloned.1.call-start = ((), (), s32[]{:S(2)}) async-start(), calls=%async_computation.3 | async-start | bytes 10485760 | tf_op jit(solution)/shard_map/all_gather | solution.py:62
  22.6 4.7 %collective-permute-start = (bf16[1,64,4096]{2,1,0:T(8,128)(2,1)}, bf16[1,64,4096]{2,1,0:T(8,128)(2,1)S(1)}, u32[]{:S(2)}, u32[]{:S(2)}) collective-permute-start(bf16[1,64,4096]{2,1,0:T(8,128)(2,1)} %get-tuple-element.11), channel_id=1, source_target_pairs={{0,1},{1,0},{2,3},{3,2},{4,5},{5,4},{6,7},{7,6},{8,9},{9,8},{10,11... | collective-permute-start | bytes 1572872 | tf_op jit(solution)/shard_map/ppermute | solution.py:27
  22.6 15.2 %collective-permute-start.1 = (bf16[1,64,4096]{2,1,0:T(8,128)(2,1)}, bf16[1,64,4096]{2,1,0:T(8,128)(2,1)S(1)}, u32[]{:S(2)}, u32[]{:S(2)}) collective-permute-start(bf16[1,64,4096]{2,1,0:T(8,128)(2,1)} %get-tuple-element.10), channel_id=1, source_target_pairs={{0,2},{1,3},{2,0},{3,1},{4,6},{5,7},{6,4},{7,5},{8,10},{9,11},{10,... | collective-permute-start | bytes 1572872 | tf_op jit(solution)/shard_map/ppermute | solution.py:27
  25.2 24.2 %collective-permute-start.2 = (bf16[1,64,4096]{2,1,0:T(8,128)(2,1)}, bf16[1,64,4096]{2,1,0:T(8,128)(2,1)S(1)}, u32[]{:S(2)}, u32[]{:S(2)}) collective-permute-start(bf16[1,64,4096]{2,1,0:T(8,128)(2,1)} %get-tuple-element.9), channel_id=1, source_target_pairs={{0,3},{1,2},{2,1},{3,0},{4,7},{5,6},{6,5},{7,4},{8,11},{9,10},{10,... | collective-permute-start | bytes 1572872 | tf_op jit(solution)/shard_map/ppermute | solution.py:27
  25.2 25.1 %collective-permute-start.3 = (bf16[1,64,4096]{2,1,0:T(8,128)(2,1)}, bf16[1,64,4096]{2,1,0:T(8,128)(2,1)S(1)}, u32[]{:S(2)}, u32[]{:S(2)}) collective-permute-start(bf16[1,64,4096]{2,1,0:T(8,128)(2,1)} %get-tuple-element.8), channel_id=1, source_target_pairs={{0,4},{1,5},{2,6},{3,7},{4,0},{5,1},{6,2},{7,3},{8,12},{9,13},{10,... | collective-permute-start | bytes 1572872 | tf_op jit(solution)/shard_map/ppermute | solution.py:27
  26.9 46.5 %collective-permute-start.4 = (bf16[1,64,4096]{2,1,0:T(8,128)(2,1)}, bf16[1,64,4096]{2,1,0:T(8,128)(2,1)S(1)}, u32[]{:S(2)}, u32[]{:S(2)}) collective-permute-start(bf16[1,64,4096]{2,1,0:T(8,128)(2,1)} %get-tuple-element.7), channel_id=1, source_target_pairs={{0,5},{1,4},{2,7},{3,6},{4,1},{5,0},{6,3},{7,2},{8,13},{9,12},{10,... | collective-permute-start | bytes 1572872 | tf_op jit(solution)/shard_map/ppermute | solution.py:27
  27.3 46.9 %collective-permute-start.5 = (bf16[1,64,4096]{2,1,0:T(8,128)(2,1)}, bf16[1,64,4096]{2,1,0:T(8,128)(2,1)S(1)}, u32[]{:S(2)}, u32[]{:S(2)}) collective-permute-start(bf16[1,64,4096]{2,1,0:T(8,128)(2,1)} %get-tuple-element.6), channel_id=1, source_target_pairs={{0,6},{1,7},{2,4},{3,5},{4,2},{5,3},{6,0},{7,1},{8,14},{9,15},{10,... | collective-permute-start | bytes 1572872 | tf_op jit(solution)/shard_map/ppermute | solution.py:27
  37.8 37.3 %collective-permute-start.6 = (bf16[1,64,4096]{2,1,0:T(8,128)(2,1)S(1)}, bf16[1,64,4096]{2,1,0:T(8,128)(2,1)S(1)}, u32[]{:S(2)}, u32[]{:S(2)}) collective-permute-start(bf16[1,64,4096]{2,1,0:T(8,128)(2,1)S(1)} %get-tuple-element.5), channel_id=1, source_target_pairs={{0,7},{1,6},{2,5},{3,4},{4,3},{5,2},{6,1},{7,0},{8,15},{9,14},{10,... | collective-permute-start | bytes 1572872 | tf_op jit(solution)/shard_map/ppermute | solution.py:27
  94.2 205.1 %all-to-all-start.1 = ((bf16[512,4,1024]{2,0,1:T(8,128)(2,1)}), bf16[512,4,1024]{2,0,1:T(8,128)(2,1)}, u32[]{:S(2)}, u32[]{:S(2)}) async-start(bf16[512,4,1024]{2,0,1:T(8,128)(2,1)} %copy.10), calls=%async_computation.1 | async-start | bytes 8388608 | tf_op jit(solution)/shard_map/all_to_all | solution.py:76
  310.0 63.1 %collective-permute-start.7 = (bf16[1024,1024]{1,0:T(8,128)(2,1)}, bf16[1024,1024]{1,0:T(8,128)(2,1)S(1)}, u32[]{:S(2)}, u32[]{:S(2)}) collective-permute-start(bf16[1024,1024]{1,0:T(8,128)(2,1)} %get-tuple-element.13), channel_id=1, source_target_pairs={{0,8},{8,0},{16,24},{24,16},{1,9},{9,1},{17,25},{25,17},{2,10},{10... | collective-permute-start | bytes 6291464 | tf_op jit(solution)/shard_map/ppermute | solution.py:35
  390.2 52.8 %all-to-all-start = ((bf16[8,64,1024]{2,1,0:T(8,128)(2,1)}), bf16[8,64,1024]{2,1,0:T(8,128)(2,1)S(1)}, u32[]{:S(2)}, u32[]{:S(2)}) async-start(bf16[8,64,1024]{2,1,0:T(8,128)(2,1)} %bitcast.25), calls=%async_computation | async-start | bytes 2097152 | tf_op jit(solution)/shard_map/all_to_all | solution.py:66
  394.7 33.1 %copy-start = (f32[1024,1024]{1,0:T(8,128)S(1)}, f32[1024,1024]{1,0:T(8,128)}, u32[]{:S(2)}) copy-start(f32[1024,1024]{1,0:T(8,128)} %get-tuple-element.3) | copy-start | bytes 12582916
  394.8 33.1 %copy-start.1 = (f32[1024,1024]{1,0:T(8,128)S(1)}, f32[1024,1024]{1,0:T(8,128)}, u32[]{:S(2)}) copy-start(f32[1024,1024]{1,0:T(8,128)} %get-tuple-element.4) | copy-start | bytes 12582916
  394.8 33.1 %copy-start.2 = (f32[1,512,1024]{2,1,0:T(8,128)S(1)}, f32[1,512,1024]{2,1,0:T(8,128)}, u32[]{:S(2)}) copy-start(f32[1,512,1024]{2,1,0:T(8,128)} %param.10) | copy-start | bytes 6291460
Sparse Core Ops, SparseCore 0:
  9.5 82.6 all-gather.3
  93.8 234.6 all-gather.5
